TPU v7x, 256 devices: a whole 4x4x8 slice. The times are simulated.
256 devices in a mesh: mp: 4 (over z_lo, core), fsdp: 16 (over y, x), dp: 4 (over z_hi).
Axes of the slice: x: 4, y: 4, z: 8 (z_hi: 4, z_lo: 2; z = z_hi * 2 + z_lo), core: 2. Of those that a mesh axis runs over, the one named last changes fastest.
Arguments:
- gen_noise: float32 [4, 4096, 128], P('dp', 'fsdp'), may hold values from -6 to 6
- renoise: float32 [4, 4096, 128], P('dp', 'fsdp'), may hold values from -120 to 120
- gen_step: int32 [4], P('dp'), may hold values from 250 to 999
- renoise_step: int32 [4], P('dp'), may hold values from 20 to 979
- text_pooled: bfloat16 [4, 768], P('dp'), may hold values from -6 to 6
- embed: bfloat16 [3, 64, 3072], replicated, may hold values from -0.75 to 0.75
- mod_weight: bfloat16 [3, 1024, 6144], P(None, None, 'fsdp'), may hold values from -0.1875 to 0.1875
- proj_weight: bfloat16 [3, 3072, 3072], P(None, 'fsdp', 'mp'), may hold values from -0.109375 to 0.109375
- unembed: bfloat16 [3, 64, 3072], P(None, None, 'mp'), may hold values from -0.109375 to 0.109375
Outputs:
- gen_grad: float32 [3072, 3072], P('fsdp', 'mp')
- score_gap: float32 [4, 4096, 128], P('dp', 'fsdp')
All inputs are finite; a program needn't handle non-finite values. Where the computation divides by a largest or mean magnitude, that divisor is 1e-20 or more.
Results may differ from a plain program's by a relative error of at most 0.03.
Values may be sent and summed in bfloat16 or wider, within the bound.
A program may use at most 128 MiB of HBM per device.

v0:
```python
import math
import jax
import jax.numpy as jnp
from jax import lax
from jax.sharding import PartitionSpec as P

D = 3072
CH = 64
TEMB = 256
GUIDANCE = 3.5
EPS_NORM = 1e-06
EPS_GAP = 1e-05
HIGH = lax.Precision.HIGHEST


def sinusoid(timesteps):
    half_size = TEMB // 2
    frequency = jnp.exp(-math.log(10000.0) * jnp.arange(half_size, dtype=jnp.float32) / half_size)
    angles = timesteps.astype(jnp.float32)[:, None] * frequency[None, :]
    return jnp.concatenate([jnp.cos(angles), jnp.sin(angles)], axis=1)


def condition(timesteps, pooled):
    joined = jnp.concatenate([sinusoid(timesteps), pooled.astype(jnp.float32)], axis=1)
    return jax.nn.silu(joined).astype(jnp.bfloat16)


def mm(left, right):
    return jnp.dot(left, right, precision=HIGH, preferred_element_type=jnp.float32)


def doubled(block):
    zero = jnp.zeros_like(block)
    return jnp.concatenate(
        [jnp.concatenate([block, zero], axis=1), jnp.concatenate([zero, block], axis=1)], axis=0
    )


def body(
    gen_noise, renoise, gen_step, renoise_step, text_pooled, embed, mod_weight, proj_weight, unembed
):
    rows = proj_weight.shape[1]
    quarter = proj_weight.shape[2]
    fsdp_size = lax.axis_size("fsdp")
    row_start = lax.axis_index("fsdp") * rows
    col_start = lax.axis_index("mp") * quarter
    noisy_vec = condition(renoise_step, text_pooled)
    blank_vec = condition(renoise_step, jnp.zeros_like(text_pooled))
    gen_vec = condition(gen_step, text_pooled)
    teacher = jnp.dot(
        jnp.concatenate([noisy_vec, blank_vec], axis=0),
        mod_weight[1],
        preferred_element_type=jnp.float32,
    )
    local_mod = jnp.concatenate(
        [
            jnp.dot(gen_vec, mod_weight[0], preferred_element_type=jnp.float32),
            teacher[1:] + GUIDANCE * (teacher[:1] - teacher[1:]),
            jnp.dot(noisy_vec, mod_weight[2], preferred_element_type=jnp.float32),
        ],
        axis=0,
    )
    modulation = lax.all_gather(local_mod, "fsdp", axis=1, tiled=True)
    shift = lax.dynamic_slice_in_dim(modulation, row_start, rows, 1)
    gain = 1.0 + lax.dynamic_slice_in_dim(modulation, D + row_start, rows, 1)
    wide = embed.astype(jnp.float32)
    centred = wide - jnp.mean(wide, axis=2, keepdims=True)
    spread = jnp.einsum("mcd,med->mce", centred, centred, precision=HIGH) / D
    mine = lax.dynamic_slice_in_dim(centred, row_start, rows, 2)
    folded = jnp.einsum("mrk,mok->mro", proj_weight, unembed, preferred_element_type=jnp.float32)
    maps = jnp.einsum("mcr,mro->mco", mine * gain[:, None, :], folded, precision=HIGH)
    offsets = jnp.einsum("mr,mro->mo", shift, folded, precision=HIGH)
    own_cols = lax.dynamic_slice_in_dim(embed, col_start, quarter, 2)
    direct = (
        jnp.einsum("mck,mok->mco", own_cols, unembed, preferred_element_type=jnp.float32)
        / fsdp_size
    )
    total = lax.psum(jnp.concatenate([maps, direct, offsets[:, None, :]], axis=1), ("fsdp", "mp"))
    maps, direct, offsets = (total[:, :CH], total[:, CH : 2 * CH], total[:, 2 * CH :])
    halves = doubled(jnp.ones((CH, CH), jnp.float32))

    def inverse_std(values, which):
        energy = mm(values, doubled(spread[which])) * values
        return lax.rsqrt(jnp.maximum(mm(energy, halves), 0.0) + EPS_NORM)

    def predict(values, scale, which):
        offset = jnp.concatenate([offsets[which], offsets[which]], axis=1)
        return (
            mm(values, doubled(direct[which])) + scale * mm(values, doubled(maps[which])) + offset
        )

    latent = gen_noise[0].astype(jnp.bfloat16).astype(jnp.float32)
    gen_scale = inverse_std(latent, 0)
    clean_lat = predict(latent, gen_scale, 0)
    noise_level = renoise_step[0].astype(jnp.float32) / 1000.0
    noisy_lat = (1.0 - noise_level) * clean_lat + noise_level * renoise[0]
    noisy = noisy_lat.astype(jnp.bfloat16).astype(jnp.float32)
    real_out = predict(noisy, inverse_std(noisy, 1), 1)
    fake_out = predict(noisy, inverse_std(noisy, 2), 2)
    real_pred = noisy_lat - noise_level * real_out
    raw_gap = noise_level * (real_out - fake_out)
    moment = lax.dot_general(
        (gen_scale * latent).astype(jnp.bfloat16),
        raw_gap.astype(jnp.bfloat16),
        (((0,), (0,)), ((), ())),
        preferred_element_type=jnp.float32,
    )
    moment = moment[:CH, :CH] + moment[CH:, CH:]
    sums = jnp.sum(raw_gap, axis=0)
    sums = sums[:CH] + sums[CH:]
    distance = jnp.full((1, CH), jnp.sum(jnp.abs(clean_lat - real_pred)))
    reduced = lax.psum(jnp.concatenate([moment, sums[None], distance], axis=0), "fsdp")
    seq_len = 2 * gen_noise.shape[1] * fsdp_size
    gap_scale = reduced[CH + 1, 0] / (seq_len * CH) + EPS_GAP
    score_gap = raw_gap / gap_scale
    moment = reduced[: CH + 1] / (gap_scale * math.sqrt(seq_len * lax.axis_size("dp")))
    left = jnp.concatenate([mine[0] * gain[0][None], shift[:1]], axis=0)
    term = lax.dot_general(
        left, moment, (((0,), (0,)), ((), ())), precision=HIGH, preferred_element_type=jnp.float32
    )
    term = lax.psum(term, "dp")
    gen_grad = mm(term, unembed[0].astype(jnp.float32))
    return (gen_grad, score_gap[None])


def solution(mesh):
    return jax.shard_map(
        body,
        mesh=mesh,
        in_specs=(
            P("dp", "fsdp", None),
            P("dp", "fsdp", None),
            P("dp"),
            P("dp"),
            P("dp", None),
            P(),
            P(None, None, "fsdp"),
            P(None, "fsdp", "mp"),
            P(None, None, "mp"),
        ),
        out_specs=(P("fsdp", "mp"), P("dp", "fsdp", None)),
        check_vma=False,
    )
```

profile of v0, /device:TPU:32, one launch (start us, length us, event | category | flops | bytes accessed | tf_op | source)
XLA Modules:
  0.0 649.7 jit_solution(15895108352038117610)
XLA Ops:
  7.2 0.0 copy-start
  7.2 0.0 copy-start.1
  7.2 0.0 all-reduce.20.cloned.1.call-start
  7.2 0.8 convert_reduce_fusion.1
  8.1 0.7 convert_element_type.74
  9.5 0.1 fusion.137
  10.3 1.3 fusion.14
  11.7 1.3 fusion.16
  13.1 1.3 fusion.18
  14.4 0.1 pad_maximum_fusion.1
  14.4 23.9 %all_gather.3 = f32[3,6144]{1,0:T(4,128)S(1)} all-gather(f32[3,384]{1,0:T(4,128)S(1)} %pad_maximum_fusion.1), channel_id=1, replica_groups=mesh['mp'=4,'fsdp'=16,'dp'=4] {'fsdp'}, dimensions={1}, use_global_device_ids=true | all-gather | bytes 78336 | tf_op jit(solution)/shard_map/all_gather | solution.py:63
  38.4 0.0 copy-done.1
  38.4 0.0 copy-start.2
  38.4 0.2 convert_reduce_fusion
  38.6 1.7 convert_subtract_fusion
  40.3 0.0 copy-done
  40.3 0.0 copy-done.2
  40.3 0.4 fusion.140
  40.7 0.0 copy-start.5
  40.8 0.2 convolution_multiply_fusion.5
  41.0 0.0 copy-start.3
  41.0 0.1 dynamic-slice_bitcast_fusion.1
  41.1 0.3 fusion.96
  41.4 1.4 fusion.24
  42.8 0.0 copy-start.4
  42.8 0.8 pad_maximum_fusion
  43.6 0.0 all-reduce.20.cloned.1.call-update
  43.7 2.6 convolution_multiply_fusion.4
  46.3 1.0 fusion.66
  47.3 0.0 copy-done.5
  47.3 0.3 fusion.2
  47.6 0.0 copy-done.3
  47.6 0.3 fusion.4
  47.9 0.1 constant_dynamic-slice_fusion
  48.0 492.4 %all-reduce.20.cloned.1.call-done = f32[3,129,64]{1,2,0:T(8,128)} async-done(((f32[3,129,64]{1,2,0:T(8,128)}), f32[3,129,64]{1,2,0:T(8,128)}) %all-reduce.20.cloned.1.call-update) | async-done | bytes 99088 | tf_op jit(solution)/shard_map/psum | solution.py:78
  540.4 0.9 slice_reduce_fusion
  541.3 0.1 maximum_bitcast_fusion
  541.4 0.1 maximum_bitcast_fusion.1
  541.5 1.0 slice_bitcast_fusion.2
  542.5 0.3 fusion
  542.8 0.0 copy-done.4
  542.8 0.3 fusion.28
  543.1 0.3 convolution_multiply_fusion.3
  543.3 0.3 fusion.8
  543.6 0.1 maximum_bitcast_fusion.2
  543.7 0.3 convolution_multiply_fusion.1
  544.0 0.3 fusion.13
  544.2 0.3 convolution_multiply_fusion.2
  544.6 0.3 convolution_multiply_fusion
  544.9 0.9 abs_reduce_fusion
  545.8 0.3 fusion.139
  546.1 0.1 add_bitcast_fusion
  546.2 0.1 copy.17
  546.3 0.2 fusion.37
  546.5 0.1 slice_add_fusion
  546.6 0.7 pad.20.clone
  547.3 0.1 maximum_maximum_fusion
  547.4 71.8 %psum.22 = f32[66,64]{0,1:T(8,128)S(1)} all-reduce(f32[66,64]{0,1:T(8,128)S(1)} %maximum_maximum_fusion), channel_id=1, replica_groups=mesh['mp'=4,'fsdp'=16,'dp'=4] {'fsdp'}, use_global_device_ids=true, to_apply=%region_4.5 | all-reduce | flops 4224 | bytes 33792 | tf_op jit(solution)/shard_map/psum | solution.py:112
  619.1 0.6 slice.142
  620.4 0.7 divide_bitcast_fusion
  621.0 0.3 fusion.33
  621.4 20.3 %psum.23 = f32[192,64]{1,0:T(8,128)S(1)} all-reduce(f32[192,64]{1,0:T(8,128)S(1)} %fusion.33), channel_id=1, replica_groups=mesh['mp'=4,'fsdp'=16,'dp'=4] {'dp'}, use_global_device_ids=true, to_apply=%region_5.6 | all-reduce | flops 12288 | bytes 98304 | tf_op jit(solution)/shard_map/psum | solution.py:121
  641.7 1.2 fusion.29
  (13 shorter events, 0.3 us)
Async XLA Ops:
  7.2 33.2 %copy-start = (bf16[3,192,768]{2,1,0:T(8,128)(2,1)S(1)}, bf16[3,192,768]{2,1,0:T(8,128)(2,1)}, u32[]{:S(2)}) copy-start(bf16[3,192,768]{2,1,0:T(8,128)(2,1)} %param.16) | copy-start | bytes 2654212
  7.2 31.2 %copy-start.1 = (bf16[3,64,3072]{2,1,0:T(8,128)(2,1)S(1)}, bf16[3,64,3072]{2,1,0:T(8,128)(2,1)}, u32[]{:S(2)}) copy-start(bf16[3,64,3072]{2,1,0:T(8,128)(2,1)} %param.14) | copy-start | bytes 3538948
  7.2 533.2 %all-reduce.20.cloned.1.call-start = ((), (), s32[]{:S(2)}) async-start(), calls=%async_computation | async-start | bytes 393216 | tf_op jit(solution)/shard_map/psum | solution.py:78
  38.4 2.0 copy-start.2
  40.7 6.5 %copy-start.5 = (f32[1,256,128]{2,1,0:T(8,128)S(1)}, f32[1,256,128]{2,1,0:T(8,128)}, u32[]{:S(2)}) copy-start(f32[1,256,128]{2,1,0:T(8,128)} %param.9) | copy-start | bytes 393220
  41.0 6.6 %copy-start.3 = (f32[128,128]{1,0:T(8,128)S(1)}, f32[128,128]{1,0:T(8,128)}, u32[]{:S(2)}) copy-start(f32[128,128]{1,0:T(8,128)} %constant.68.clone.1) | copy-start | bytes 196612
  42.8 499.9 %copy-start.4 = (f32[1,256,128]{2,1,0:T(8,128)S(1)}, f32[1,256,128]{2,1,0:T(8,128)}, u32[]{:S(2)}) copy-start(f32[1,256,128]{2,1,0:T(8,128)} %param.10) | copy-start | bytes 393220
Sparse Core Ops, SparseCore 0:
  43.8 496.5 all-reduce.19
where the time goes:
time: 650 us
  waiting for transfers between devices  492 us (76%)
  blocking collectives  116 us (18%)
  between operations  16.4 us (3%)
  matrix products  14.6 us (2%)
  other arithmetic  6.78 us (1%)
    psum x1, waiting for transfers between devices, body(): lax.psum(jnp.concatenate([maps, direct, offsets[:, None, :]], axis=1), ('...  492 us
    psum x1, blocking collectives, body(): lax.psum(jnp.concatenate([moment, sums[None], distance], axis=0), 'fsdp')  71.8 us
    all_gather x1, blocking collectives, body(): modulation = lax.all_gather(local_mod, 'fsdp', axis=1, tiled=True)  23.9 us
    psum x1, blocking collectives, body(): term = lax.psum(term, 'dp')  20.3 us
  transfers between devices with their start and end apart: 1, of which 1 were waited for; matrix products, arithmetic and copies ran while one was open for 1% of the time, Pallas kernels for 0%

commit v1 on v0

--- a/solution.py
+++ b/solution.py
@@ -75,7 +75,9 @@
         jnp.einsum("mck,mok->mco", own_cols, unembed, preferred_element_type=jnp.float32)
         / fsdp_size
     )
-    total = lax.psum(jnp.concatenate([maps, direct, offsets[:, None, :]], axis=1), ("fsdp", "mp"))
+    total = jnp.concatenate([maps, direct, offsets[:, None, :]], axis=1)
+    for axis in ("mp", "fsdp"):
+        total = lax.psum(total, axis)
     maps, direct, offsets = (total[:, :CH], total[:, CH : 2 * CH], total[:, 2 * CH :])
     halves = doubled(jnp.ones((CH, CH), jnp.float32))
 

time: 650 us -> 292 us (0.45)
  waiting for transfers between devices: 492 us -> 134 us
    psum x1 -> x2, waiting for transfers between devices: 492 us -> 134 us  [body(): total = lax.psum(total, axis)]
  transfers between devices with their start and end apart: 1 -> 2, of which waited for: 1 -> 2; matrix products, arithmetic and copies ran while one was open for 1% -> 1% of each run, Pallas kernels for 0% -> 0%
where the time goes in v1:
time: 292 us
  waiting for transfers between devices  134 us (46%)
  blocking collectives  116 us (40%)
  between operations  16.4 us (6%)
  matrix products  14.6 us (5%)
  other arithmetic  6.78 us (2%)
  local copies, waits for them, and re-layouts  3.47 us (1%)
    psum x2, waiting for transfers between devices, body(): total = lax.psum(total, axis)  134 us
    psum x1, blocking collectives, body(): lax.psum(jnp.concatenate([moment, sums[None], distance], axis=0), 'fsdp')  72.1 us
    all_gather x1, blocking collectives, body(): modulation = lax.all_gather(local_mod, 'fsdp', axis=1, tiled=True)  23.9 us
    psum x1, blocking collectives, body(): term = lax.psum(term, 'dp')  20.3 us
  transfers between devices with their start and end apart: 2, of which 2 were waited for; matrix products, arithmetic and copies ran while one was open for 1% of the time, Pallas kernels for 0%

profile of v1, /device:TPU:32, one launch (start us, length us, event | category | flops | bytes accessed | tf_op | source)
XLA Modules:
  0.0 291.9 jit_solution(4851510147702803754)
XLA Ops:
  7.2 0.0 copy-start
  7.2 0.0 copy-start.1
  7.2 0.0 all-reduce.21.cloned.1.call-start
  7.2 0.8 convert_reduce_fusion.1
  8.1 0.7 convert_element_type.74
  9.5 0.1 fusion.137
  10.3 1.3 fusion.14
  11.7 1.3 fusion.16
  13.1 1.3 fusion.18
  14.4 0.1 pad_maximum_fusion.1
  14.4 23.9 %all_gather.3 = f32[3,6144]{1,0:T(4,128)S(1)} all-gather(f32[3,384]{1,0:T(4,128)S(1)} %pad_maximum_fusion.1), channel_id=1, replica_groups=mesh['mp'=4,'fsdp'=16,'dp'=4] {'fsdp'}, dimensions={1}, use_global_device_ids=true | all-gather | bytes 78336 | tf_op jit(solution)/shard_map/all_gather | solution.py:63
  38.4 0.0 copy-done.1
  38.4 0.0 copy-start.2
  38.4 0.2 convert_reduce_fusion
  38.6 1.7 convert_subtract_fusion
  40.3 0.0 copy-done
  40.3 0.0 copy-done.2
  40.4 0.4 fusion.140
  40.8 0.0 copy-start.3
  40.8 0.2 convolution_multiply_fusion.5
  41.0 0.1 dynamic-slice_bitcast_fusion.1
  41.1 0.3 fusion.96
  41.4 1.4 fusion.24
  42.8 0.8 pad_maximum_fusion
  43.6 0.0 all-reduce.21.cloned.1.call-update
  43.6 0.0 all-reduce.23.cloned.1.call-start
  43.7 2.6 convolution_multiply_fusion.4
  46.3 0.0 copy-done.5
  46.4 0.3 fusion.2
  46.7 0.0 copy-done.3
  46.7 0.3 fusion.4
  46.9 1.0 fusion.66
  47.9 35.8 %all-reduce.21.cloned.1.call-done = f32[3,129,64]{1,2,0:T(8,128)} async-done(((f32[3,129,64]{1,2,0:T(8,128)}), f32[3,129,64]{1,2,0:T(8,128)}) %all-reduce.21.cloned.1.call-update) | async-done | bytes 99088 | tf_op jit(solution)/shard_map/psum | solution.py:80
  83.7 0.0 all-reduce.23.cloned.1.call-update
  83.7 0.1 constant_dynamic-slice_fusion
  83.8 98.4 %all-reduce.23.cloned.1.call-done = f32[3,129,64]{1,2,0:T(8,128)} async-done(((f32[3,129,64]{1,2,0:T(8,128)}), f32[3,129,64]{1,2,0:T(8,128)}) %all-reduce.23.cloned.1.call-update) | async-done | bytes 99088 | tf_op jit(solution)/shard_map/psum | solution.py:80
  182.2 0.9 slice_reduce_fusion
  183.1 0.1 maximum_bitcast_fusion
  183.2 0.1 maximum_bitcast_fusion.1
  183.3 0.9 slice_bitcast_fusion.2
  184.2 0.3 fusion
  184.5 0.0 copy-done.4
  184.6 0.3 fusion.28
  184.9 0.3 convolution_multiply_fusion.3
  185.1 0.3 fusion.8
  185.4 0.1 maximum_bitcast_fusion.2
  185.5 0.3 convolution_multiply_fusion.1
  185.8 0.3 fusion.13
  186.0 0.3 convolution_multiply_fusion.2
  186.3 0.3 convolution_multiply_fusion
  186.7 0.9 abs_reduce_fusion
  187.6 0.3 fusion.139
  187.9 0.1 add_bitcast_fusion
  188.0 0.1 copy.17
  188.1 0.2 fusion.37
  188.3 0.1 slice_add_fusion
  188.4 0.7 pad.20.clone
  189.1 0.1 maximum_maximum_fusion
  189.2 72.1 %psum.30 = f32[66,64]{0,1:T(8,128)S(1)} all-reduce(f32[66,64]{0,1:T(8,128)S(1)} %maximum_maximum_fusion), channel_id=1, replica_groups=mesh['mp'=4,'fsdp'=16,'dp'=4] {'fsdp'}, use_global_device_ids=true, to_apply=%region_5.6 | all-reduce | flops 4224 | bytes 33792 | tf_op jit(solution)/shard_map/psum | solution.py:114
  261.3 0.6 slice.142
  262.5 0.7 divide_bitcast_fusion
  263.2 0.3 fusion.33
  263.5 20.3 %psum.31 = f32[192,64]{1,0:T(8,128)S(1)} all-reduce(f32[192,64]{1,0:T(8,128)S(1)} %fusion.33), channel_id=1, replica_groups=mesh['mp'=4,'fsdp'=16,'dp'=4] {'dp'}, use_global_device_ids=true, to_apply=%region_6.7 | all-reduce | flops 12288 | bytes 98304 | tf_op jit(solution)/shard_map/psum | solution.py:123
  283.8 1.2 fusion.29
  (15 shorter events, 0.3 us)
Async XLA Ops:
  7.2 33.2 %copy-start = (bf16[3,192,768]{2,1,0:T(8,128)(2,1)S(1)}, bf16[3,192,768]{2,1,0:T(8,128)(2,1)}, u32[]{:S(2)}) copy-start(bf16[3,192,768]{2,1,0:T(8,128)(2,1)} %param.16) | copy-start | bytes 2654212
  7.2 31.2 %copy-start.1 = (bf16[3,64,3072]{2,1,0:T(8,128)(2,1)S(1)}, bf16[3,64,3072]{2,1,0:T(8,128)(2,1)}, u32[]{:S(2)}) copy-start(bf16[3,64,3072]{2,1,0:T(8,128)(2,1)} %param.14) | copy-start | bytes 3538948
  7.2 76.5 %all-reduce.21.cloned.1.call-start = ((), (), s32[]{:S(2)}) async-start(), calls=%async_computation | async-start | bytes 393216 | tf_op jit(solution)/shard_map/psum | solution.py:80
  38.4 2.0 copy-start.2
  40.8 5.6 %copy-start.5 = (f32[1,256,128]{2,1,0:T(8,128)S(1)}, f32[1,256,128]{2,1,0:T(8,128)}, u32[]{:S(2)}) copy-start(f32[1,256,128]{2,1,0:T(8,128)} %param.9) | copy-start | bytes 393220
  40.8 5.9 %copy-start.3 = (f32[128,128]{1,0:T(8,128)S(1)}, f32[128,128]{1,0:T(8,128)}, u32[]{:S(2)}) copy-start(f32[128,128]{1,0:T(8,128)} %constant.68.clone.1) | copy-start | bytes 196612
  43.6 140.9 %copy-start.4 = (f32[1,256,128]{2,1,0:T(8,128)S(1)}, f32[1,256,128]{2,1,0:T(8,128)}, u32[]{:S(2)}) copy-start(f32[1,256,128]{2,1,0:T(8,128)} %param.10) | copy-start | bytes 393220
  43.6 138.6 %all-reduce.23.cloned.1.call-start = ((), (), s32[]{:S(2)}) async-start(), calls=%async_computation.1 | async-start | bytes 393216 | tf_op jit(solution)/shard_map/psum | solution.py:80
Sparse Core Ops, SparseCore 0:
  43.8 39.9 all-reduce.20
  87.2 94.9 all-reduce.22
